TPU v7x, 32 devices: a whole 2x2x4 slice. The times are simulated.
32 devices in a mesh: sub: 8 (over y, x, core), reg: 4 (over z).
Axes of the slice: x: 2, y: 2, z: 4, core: 2. Of those that a mesh axis runs over, the one named last changes fastest.
Arguments:
- right_side: float32 [8, 4, 1280, 16], P('sub', 'reg'), may hold values from -6 to 6
- tiles: bfloat16 [8, 4, 80, 128, 128], P('sub', 'reg'), may hold values from -1 to 5
- tile_list: int32 [8, 4, 80, 2], P('sub', 'reg'), may hold values from 0 to 9, as said below
- weights: float32 [8, 4, 1280], P('sub', 'reg'), may hold values from 0.15 to 0.35
- face_map: int32 [8, 4, 6], P('sub', 'reg'), may hold values from 0 to 9, as said below
- matching: int32 [8, 4, 6, 128], P('sub', 'reg'), may hold values from 0 to 127, each once within a row
- coarse_basis: bfloat16 [8, 4, 1280, 128], P('sub', 'reg'), may hold values from -0.15625 to 0.15625
- coarse_map: int32 [8, 4, 128], P('sub', 'reg'), may hold values from 0 to 511, as said below
- coarse_inverse: float32 [4, 512, 512], P('reg', 'sub'), may hold values from -1 to 2, as said below
Outputs:
- solution: bfloat16 [8, 4, 1280, 16], P('sub', 'reg')
- residual: bfloat16 [8, 4, 1280, 16], P('sub', 'reg')
Inputs may be any that keep to these rules, and one draw needn't show every extreme that they name: `tile_list`: entries 0 to 9 of each subdomain's list are (b, b) for b in order; the other 70 entries are distinct off-diagonal block pairs. `face_map`: the six blocks of a subdomain are distinct. `coarse_map`: A subdomain's 128 numbers are distinct, and within a subregion every number is named by exactly two subdomains. `coarse_inverse`: symmetric in its last two dimensions.
All inputs are finite; a program needn't handle non-finite values.
Results may differ from a plain program's by a relative error of at most 0.0075.
Values may be sent and summed in bfloat16 or wider, within the bound.
No kernel may reach another device: no remote copies, remote signals or barrier semaphores. Data moves between devices by JAX's collectives and lax.ppermute only.
A program may use at most 64 MiB of HBM per device.

v0:
```python
import jax
import jax.numpy as jnp
from jax import lax
from jax.sharding import PartitionSpec as P

SWEEPS = 3


def from_behind(shard, axis, by):
    peers = lax.axis_size(axis)
    return lax.ppermute(shard, axis, [(i, (i + by) % peers) for i in range(peers)])


def body(
    right_side,
    tiles,
    tile_list,
    weights,
    face_map,
    matching,
    coarse_basis,
    coarse_map,
    coarse_inverse,
):
    order = right_side.shape[2]
    rights = right_side.shape[3]
    tile = tiles.shape[3]
    blocks = order // tile
    target = right_side[0, 0]
    tile_block = tiles[0, 0]
    listing = tile_list[0, 0]
    scaling = weights[0, 0][:, None]
    faces_here = face_map[0, 0]
    matched = matching[0, 0]
    basis = coarse_basis[0, 0]
    own_map = coarse_map[0, 0]
    own_count = own_map.shape[0]
    inverse_rows = coarse_inverse[0]
    held_rows = inverse_rows.shape[0]
    block_ids = jnp.arange(blocks, dtype=jnp.int32)
    row_table = (listing[:, 0][None, :] == block_ids[:, None]).astype(jnp.float32)
    face_table = (faces_here[None, :] == block_ids[:, None]).astype(jnp.float32)
    stride = max(lax.axis_size("reg") // 4, 1)
    every_ids = lax.all_gather(own_map, "sub", axis=0, tiled=True)
    outgoing_part = jnp.take(inverse_rows, every_ids, axis=1).reshape(
        held_rows, lax.axis_size("sub"), own_count
    )
    received_part = lax.all_to_all(outgoing_part, "sub", split_axis=1, concat_axis=0, tiled=True)
    own_columns = received_part.reshape(held_rows * lax.axis_size("sub"), own_count)
    own_block = jnp.transpose(jnp.take(own_columns, every_ids, axis=0))
    solution = jnp.zeros_like(target)
    residual = target
    for sweep in range(SWEEPS):
        low = residual.astype(jnp.bfloat16)
        local_coarse = jnp.einsum("mn,mr->nr", basis, low, preferred_element_type=jnp.float32)
        own_solution = jnp.dot(
            own_block,
            lax.all_gather(local_coarse, "sub", axis=0, tiled=True),
            precision=lax.Precision.HIGHEST,
            preferred_element_type=jnp.float32,
        )
        own_values = own_solution.astype(jnp.bfloat16)
        correction = jnp.dot(basis, own_values, preferred_element_type=jnp.float32)
        solution = solution + (scaling * residual + correction)
        operator_low = solution.astype(jnp.bfloat16).reshape(blocks, tile, rights)
        picked = jnp.take(operator_low, listing[:, 1], axis=0)
        products = jnp.einsum(
            "tij,tjr->tir", tile_block, picked, preferred_element_type=jnp.float32
        )
        local = jnp.einsum("bt,tir->bir", row_table, products, precision=lax.Precision.HIGHEST)
        stacked = solution.reshape(blocks, tile, rights)
        outgoing = jnp.take(stacked, faces_here, axis=0)
        arrived = []
        for face, offset in ((0, 1), (1, -1), (2, stride), (3, -stride)):
            arrived.append(from_behind(outgoing[face ^ 1], "reg", offset))
        for face, offset in ((4, 1), (5, -1)):
            arrived.append(from_behind(outgoing[face ^ 1], "sub", offset))
        received = jnp.stack(arrived)
        permuted = jnp.take_along_axis(received, matched[:, :, None], axis=1)
        coupling = jnp.einsum("bk,kir->bir", face_table, permuted, precision=lax.Precision.HIGHEST)
        residual = target - (local - 0.5 * coupling).reshape(order, rights)
    shape = (1, 1, order, rights)
    return (
        solution.astype(jnp.bfloat16).reshape(shape),
        residual.astype(jnp.bfloat16).reshape(shape),
    )


def solution(mesh):
    placed = (
        P("sub", "reg", None, None),
        P("sub", "reg", None, None, None),
        P("sub", "reg", None, None),
        P("sub", "reg", None),
        P("sub", "reg", None),
        P("sub", "reg", None, None),
        P("sub", "reg", None, None),
        P("sub", "reg", None),
        P("reg", "sub", None),
    )
    return jax.shard_map(
        body,
        mesh=mesh,
        in_specs=placed,
        out_specs=(P("sub", "reg", None, None), P("sub", "reg", None, None)),
        check_vma=False,
    )
```

profile of v0, /device:TPU:0, one launch (start us, length us, event | category | flops | bytes accessed | tf_op | source)
XLA Modules:
  0.0 149.0 jit_solution(13466135424913627133)
XLA Ops:
  0.7 10.7 %all-gather = s32[1,1,1024]{2,1,0:T(1,128)S(1)} all-gather(s32[1,1,128]{2,1,0:T(1,128)} %param.22), channel_id=2, replica_groups=mesh['sub'=8,'reg'=4] {'sub'}, dimensions={2}, use_global_device_ids=true | all-gather | bytes 4608 | tf_op jit(solution)/shard_map/all_gather | solution.py:44
  12.4 4.0 %gather_fusion = f32[1024,64]{1,0:T(8,128)} fusion(f32[64,512]{0,1:T(8,128)S(1)} %bitcast.251, s32[1024]{0:T(1024)S(1)} %fusion.82), kind=kCustom, calls=%fused_computation.9 | custom fusion | bytes 528384 | tf_op jit(solution)/shard_map/jit(_take)/gather | solution.py:45
  18.3 3.4 %all-to-all-start = ((f32[64,8,128]{2,0,1:T(8,128)}), f32[64,8,128]{2,0,1:T(8,128)S(1)}, u32[]{:S(2)}, u32[]{:S(2)}) async-start(f32[64,8,128]{2,0,1:T(8,128)} %broadcast_select_fusion), calls=%async_computation | async-start | bytes 524288 | tf_op jit(solution)/shard_map/all_to_all | solution.py:48
  23.7 9.5 %all_gather.13 = f32[1024,16]{0,1:T(8,128)S(1)} all-gather(f32[128,16]{0,1:T(8,128)S(1)} %fusion.37), channel_id=1, replica_groups=mesh['sub'=8,'reg'=4] {'sub'}, dimensions={0}, use_global_device_ids=true | all-gather | bytes 73728 | tf_op jit(solution)/shard_map/all_gather | solution.py:58
  33.3 4.0 %gather_fusion.1 = f32[1024,128]{1,0:T(8,128)} fusion(f32[512,128]{1,0:T(8,128)S(1)} %bitcast.250, s32[1024]{0:T(1024)S(1)} %fusion.82), kind=kCustom, calls=%fused_computation.10 | custom fusion | bytes 1052672 | tf_op jit(solution)/shard_map/jit(_take)/gather | solution.py:50
  37.2 1.5 %convolution_convert_fusion.2 = bf16[128,16]{0,1:T(8,128)(2,1)S(1)} fusion(f32[1024,16]{0,1:T(8,128)S(1)} %all_gather.13, f32[1024,128]{1,0:T(8,128)} %gather_fusion.1, pred[1024]{0:T(1024)(128)(4,1)S(1)} %compare_and_fusion.1), kind=kOutput, calls=%fused_computation.38 | convolution fusion | flops 25298944 | bytes 594944 | tf_op jit(solution)/shard_map/dot_general | solution.py:56
  39.7 1.6 %collective-permute-start = (f32[128,16]{0,1:T(8,128)S(1)}, f32[128,16]{0,1:T(8,128)}, u32[]{:S(2)}, u32[]{:S(2)}) collective-permute-start(f32[128,16]{0,1:T(8,128)S(1)} %get-tuple-element.26), channel_id=1, source_target_pairs={{0,1},{1,2},{2,3},{3,0},{4,5},{5,6},{6,7},{7,4},{8,9},{9,10},{10,1... | collective-permute-start | bytes 24584 | tf_op jit(solution)/shard_map/ppermute | solution.py:11
  41.3 2.2 %collective-permute-start.1 = (f32[128,16]{0,1:T(8,128)S(1)}, f32[128,16]{0,1:T(8,128)}, u32[]{:S(2)}, u32[]{:S(2)}) collective-permute-start(f32[128,16]{0,1:T(8,128)S(1)} %get-tuple-element.25), channel_id=1, source_target_pairs={{0,3},{1,0},{2,1},{3,2},{4,7},{5,4},{6,5},{7,6},{8,11},{9,8},{10,9... | collective-permute-start | bytes 24584 | tf_op jit(solution)/shard_map/ppermute | solution.py:11
  43.6 3.8 %collective-permute-start.3 = (f32[128,16]{0,1:T(8,128)S(1)}, f32[128,16]{0,1:T(8,128)}, u32[]{:S(2)}, u32[]{:S(2)}) collective-permute-start(f32[128,16]{0,1:T(8,128)S(1)} %get-tuple-element.23), channel_id=1, source_target_pairs={{0,3},{1,0},{2,1},{3,2},{4,7},{5,4},{6,5},{7,6},{8,11},{9,8},{10,9... | collective-permute-start | bytes 24584 | tf_op jit(solution)/shard_map/ppermute | solution.py:11
  48.2 2.2 %fusion.11 = f32[80,128,16]{1,2,0:T(8,128)S(1)} fusion(bf16[1,1,80,128,128]{4,3,2,1,0:T(8,128)(2,1)S(1)} %copy-done, bf16[80,128,16]{1,2,0:T(8,128)(2,1)S(1)} %gather_fusion.2, pred[80]{0:T(512)(128)(4,1)} %get-tuple-element.4), kind=kOutput, calls=%fused_computation.25 | convolution fusion | flops 42106880 | bytes 3604560 | tf_op jit(solution)/shard_map/tij,tjr->tir/dot_general | solution.py:67
  51.5 2.6 %collective-permute-start.5 = (f32[128,16]{0,1:T(8,128)S(1)}, f32[128,16]{0,1:T(8,128)S(1)}, u32[]{:S(2)}, u32[]{:S(2)}) collective-permute-start(f32[128,16]{0,1:T(8,128)S(1)} %get-tuple-element.21), channel_id=1, source_target_pairs={{0,28},{4,0},{8,4},{12,8},{16,12},{20,16},{24,20},{28,24},{1,29},{... | collective-permute-start | bytes 24584 | tf_op jit(solution)/shard_map/ppermute | solution.py:11
  54.2 1.3 constant_dynamic-update-slice_fusion.5
  55.5 1.3 constant_dynamic-update-slice_fusion.4
  56.8 1.3 constant_dynamic-update-slice_fusion.3
  59.4 1.3 constant_dynamic-update-slice_fusion.1
  62.2 7.0 %gather_fusion.4 = f32[768,16]{1,0:T(8,128)} fusion(f32[6,128,16]{2,1,0:T(8,128)S(1)} %copy.35, s32[768]{0:T(1024)S(1)} %bitcast.246), kind=kCustom, calls=%fused_computation.2.clone | custom fusion | bytes 104448 | tf_op jit(solution)/shard_map/jit(take_along_axis)/gather | solution.py:79
  71.8 9.0 %all_gather.14 = f32[1024,16]{0,1:T(8,128)S(1)} all-gather(f32[128,16]{0,1:T(8,128)S(1)} %convolution_bitcast_fusion.4), channel_id=1, replica_groups=mesh['sub'=8,'reg'=4] {'sub'}, dimensions={0}, use_global_device_ids=true | all-gather | bytes 73728 | tf_op jit(solution)/shard_map/all_gather | solution.py:58
  80.8 1.5 %convolution_convert_fusion.1 = bf16[128,16]{0,1:T(8,128)(2,1)S(1)} fusion(f32[1024,16]{0,1:T(8,128)S(1)} %all_gather.14, f32[1024,128]{1,0:T(8,128)} %gather_fusion.1, pred[1024]{0:T(1024)(128)(4,1)S(1)} %compare_and_fusion.1), kind=kOutput, calls=%fused_computation.37 | convolution fusion | flops 25298944 | bytes 594944 | tf_op jit(solution)/shard_map/dot_general | solution.py:56
  84.2 2.4 %fusion.14 = f32[80,128,16]{1,2,0:T(8,128)} fusion(bf16[1,1,80,128,128]{4,3,2,1,0:T(8,128)(2,1)S(1)} %copy-done, bf16[80,128,16]{1,2,0:T(8,128)(2,1)S(1)} %gather_fusion.5, pred[80]{0:T(512)(128)(4,1)S(1)} %copy-done.13), kind=kOutput, calls=%fused_computation.26 | convolution fusion | flops 42106880 | bytes 3604560 | tf_op jit(solution)/shard_map/tij,tjr->tir/dot_general | solution.py:67
  87.3 2.2 %fusion.25 = f32[10,128,16]{1,0,2:T(8,128)} fusion(f32[80,128,16]{1,2,0:T(8,128)} %fusion.14, s32[80]{0:T(128)S(1)} %copy-done.12), kind=kOutput, calls=%fused_computation.41 | convolution fusion | flops 19661600 | bytes 737600 | tf_op jit(solution)/shard_map/bt,tir->bir/dot_general | solution.py:70
  89.5 3.8 %collective-permute-start.7 = (f32[128,16]{0,1:T(8,128)S(1)}, f32[128,16]{0,1:T(8,128)S(1)}, u32[]{:S(2)}, u32[]{:S(2)}) collective-permute-start(f32[128,16]{0,1:T(8,128)S(1)} %get-tuple-element.19), channel_id=1, source_target_pairs={{0,3},{1,0},{2,1},{3,2},{4,7},{5,4},{6,5},{7,6},{8,11},{9,8},{10,9... | collective-permute-start | bytes 24584 | tf_op jit(solution)/shard_map/ppermute | solution.py:11
  93.3 3.8 %collective-permute-start.9 = (f32[128,16]{0,1:T(8,128)S(1)}, f32[128,16]{0,1:T(8,128)S(1)}, u32[]{:S(2)}, u32[]{:S(2)}) collective-permute-start(f32[128,16]{0,1:T(8,128)S(1)} %get-tuple-element.17), channel_id=1, source_target_pairs={{0,3},{1,0},{2,1},{3,2},{4,7},{5,4},{6,5},{7,6},{8,11},{9,8},{10,9... | collective-permute-start | bytes 24584 | tf_op jit(solution)/shard_map/ppermute | solution.py:11
  97.1 2.6 %collective-permute-start.11 = (f32[128,16]{0,1:T(8,128)S(1)}, f32[128,16]{0,1:T(8,128)S(1)}, u32[]{:S(2)}, u32[]{:S(2)}) collective-permute-start(f32[128,16]{0,1:T(8,128)S(1)} %get-tuple-element.15), channel_id=1, source_target_pairs={{0,28},{4,0},{8,4},{12,8},{16,12},{20,16},{24,20},{28,24},{1,29},{... | collective-permute-start | bytes 24584 | tf_op jit(solution)/shard_map/ppermute | solution.py:11
  101.3 7.0 %gather_fusion.7 = f32[768,16]{1,0:T(8,128)} fusion(f32[6,128,16]{2,1,0:T(8,128)S(1)} %copy.40, s32[768]{0:T(1024)S(1)} %bitcast.247), kind=kCustom, calls=%fused_computation.7.clone | custom fusion | bytes 104448 | tf_op jit(solution)/shard_map/jit(take_along_axis)/gather | solution.py:79
  110.9 9.3 %all_gather.15 = f32[1024,16]{0,1:T(8,128)S(1)} all-gather(f32[128,16]{0,1:T(8,128)S(1)} %convolution_bitcast_fusion.3), channel_id=1, replica_groups=mesh['sub'=8,'reg'=4] {'sub'}, dimensions={0}, use_global_device_ids=true | all-gather | bytes 73728 | tf_op jit(solution)/shard_map/all_gather | solution.py:58
  120.2 1.5 %convolution_convert_fusion = bf16[128,16]{0,1:T(8,128)(2,1)S(1)} fusion(f32[1024,16]{0,1:T(8,128)S(1)} %all_gather.15, f32[1024,128]{1,0:T(8,128)} %gather_fusion.1, pred[1024]{0:T(1024)(128)(4,1)S(1)} %compare_and_fusion.1), kind=kOutput, calls=%fused_computation.36 | convolution fusion | flops 25298944 | bytes 594944 | tf_op jit(solution)/shard_map/dot_general | solution.py:56
  123.4 2.4 %fusion.17 = f32[80,128,16]{1,2,0:T(8,128)} fusion(bf16[1,1,80,128,128]{4,3,2,1,0:T(8,128)(2,1)S(1)} %copy-done, bf16[80,128,16]{1,2,0:T(8,128)(2,1)S(1)} %gather_fusion.8, pred[80]{0:T(512)(128)(4,1)S(1)} %copy-done.13), kind=kOutput, calls=%fused_computation.27 | convolution fusion | flops 42106880 | bytes 3604560 | tf_op jit(solution)/shard_map/tij,tjr->tir/dot_general | solution.py:67
  126.4 1.6 %fusion.23 = f32[10,128,16]{1,0,2:T(8,128)S(1)} fusion(f32[80,128,16]{1,2,0:T(8,128)} %fusion.17, s32[80]{0:T(128)S(1)} %copy-done.12), kind=kOutput, calls=%fused_computation.39 | convolution fusion | flops 19661600 | bytes 737600 | tf_op jit(solution)/shard_map/bt,tir->bir/dot_general | solution.py:70
  128.0 3.9 %collective-permute-start.13 = (f32[128,16]{0,1:T(8,128)S(1)}, f32[128,16]{0,1:T(8,128)S(1)}, u32[]{:S(2)}, u32[]{:S(2)}) collective-permute-start(f32[128,16]{0,1:T(8,128)S(1)} %get-tuple-element.13), channel_id=1, source_target_pairs={{0,3},{1,0},{2,1},{3,2},{4,7},{5,4},{6,5},{7,6},{8,11},{9,8},{10,9... | collective-permute-start | bytes 24584 | tf_op jit(solution)/shard_map/ppermute | solution.py:11
  131.9 3.8 %collective-permute-start.15 = (f32[128,16]{0,1:T(8,128)S(1)}, f32[128,16]{0,1:T(8,128)S(1)}, u32[]{:S(2)}, u32[]{:S(2)}) collective-permute-start(f32[128,16]{0,1:T(8,128)S(1)} %get-tuple-element.11), channel_id=1, source_target_pairs={{0,3},{1,0},{2,1},{3,2},{4,7},{5,4},{6,5},{7,6},{8,11},{9,8},{10,9... | collective-permute-start | bytes 24584 | tf_op jit(solution)/shard_map/ppermute | solution.py:11
  135.7 2.6 %collective-permute-start.17 = (f32[128,16]{0,1:T(8,128)S(1)}, f32[128,16]{0,1:T(8,128)S(1)}, u32[]{:S(2)}, u32[]{:S(2)}) collective-permute-start(f32[128,16]{0,1:T(8,128)S(1)} %get-tuple-element.9), channel_id=1, source_target_pairs={{0,28},{4,0},{8,4},{12,8},{16,12},{20,16},{24,20},{28,24},{1,29},{... | collective-permute-start | bytes 24584 | tf_op jit(solution)/shard_map/ppermute | solution.py:11
  139.9 7.0 %gather_fusion.10 = f32[768,16]{1,0:T(8,128)} fusion(f32[6,128,16]{2,1,0:T(8,128)S(1)} %copy.45, s32[768]{0:T(1024)S(1)} %bitcast.248), kind=kCustom, calls=%fused_computation.8.clone | custom fusion | bytes 104448 | tf_op jit(solution)/shard_map/jit(take_along_axis)/gather | solution.py:79
  (125 shorter events, 25.8 us)
Async XLA Ops:
  0.6 47.6 %copy-start = (bf16[1,1,80,128,128]{4,3,2,1,0:T(8,128)(2,1)S(1)}, bf16[1,1,80,128,128]{4,3,2,1,0:T(8,128)(2,1)}, u32[]{:S(2)}) copy-start(bf16[1,1,80,128,128]{4,3,2,1,0:T(8,128)(2,1)} %param.16) | copy-start | bytes 7864324
  0.6 21.1 %copy-start.14 = (s32[1,1,80,2]{2,3,1,0:T(2,128)S(1)}, s32[1,1,80,2]{2,3,1,0:T(2,128)}, u32[]{:S(2)}) copy-start(s32[1,1,80,2]{2,3,1,0:T(2,128)} %param.17) | copy-start | bytes 1924
  0.7 22.2 %copy-start.7 = (s32[1,1,6]{2,1,0:T(1,128)S(1)}, s32[1,1,6]{2,1,0:T(1,128)}, u32[]{:S(2)}) copy-start(s32[1,1,6]{2,1,0:T(1,128)} %param.19) | copy-start | bytes 76
  0.7 22.2 %copy-start.5 = (s32[1,1,6,128]{3,1,2,0:T(1,128)S(1)}, s32[1,1,6,128]{3,1,2,0:T(1,128)}, u32[]{:S(2)}) copy-start(s32[1,1,6,128]{3,1,2,0:T(1,128)} %param.20) | copy-start | bytes 9220
  0.7 22.2 %copy-start.1 = (bf16[1,1,1280,128]{3,2,1,0:T(8,128)(2,1)S(1)}, bf16[1,1,1280,128]{3,2,1,0:T(8,128)(2,1)}, u32[]{:S(2)}) copy-start(bf16[1,1,1280,128]{3,2,1,0:T(8,128)(2,1)} %param.21) | copy-start | bytes 983044
  0.7 22.2 %copy-start.2 = (f32[1,1,1280,16]{2,3,1,0:T(8,128)S(1)}, f32[1,1,1280,16]{2,3,1,0:T(8,128)}, u32[]{:S(2)}) copy-start(f32[1,1,1280,16]{2,3,1,0:T(8,128)} %param.15) | copy-start | bytes 245764
  0.7 32.5 %copy-start.6 = (f32[1,1,1280]{2,1,0:T(1,128)S(1)}, f32[1,1,1280]{2,1,0:T(1,128)}, u32[]{:S(2)}) copy-start(f32[1,1,1280]{2,1,0:T(1,128)} %param.18) | copy-start | bytes 15364
  18.3 14.9 %all-to-all-start = ((f32[64,8,128]{2,0,1:T(8,128)}), f32[64,8,128]{2,0,1:T(8,128)S(1)}, u32[]{:S(2)}, u32[]{:S(2)}) async-start(f32[64,8,128]{2,0,1:T(8,128)} %broadcast_select_fusion), calls=%async_computation | async-start | bytes 524288 | tf_op jit(solution)/shard_map/all_to_all | solution.py:48
  22.9 16.7 %copy-start.9 = (pred[6]{0:T(512)(128)(4,1)}, pred[6]{0:T(512)(128)(4,1)S(1)}, u32[]{:S(2)}) copy-start(pred[6]{0:T(512)(128)(4,1)S(1)} %compare_and_fusion.2) | copy-start | bytes 22
  39.7 11.8 %collective-permute-start = (f32[128,16]{0,1:T(8,128)S(1)}, f32[128,16]{0,1:T(8,128)}, u32[]{:S(2)}, u32[]{:S(2)}) collective-permute-start(f32[128,16]{0,1:T(8,128)S(1)} %get-tuple-element.26), channel_id=1, source_target_pairs={{0,1},{1,2},{2,3},{3,0},{4,5},{5,6},{6,7},{7,4},{8,9},{9,10},{10,1... | collective-permute-start | bytes 24584 | tf_op jit(solution)/shard_map/ppermute | solution.py:11
  41.3 14.2 %collective-permute-start.1 = (f32[128,16]{0,1:T(8,128)S(1)}, f32[128,16]{0,1:T(8,128)}, u32[]{:S(2)}, u32[]{:S(2)}) collective-permute-start(f32[128,16]{0,1:T(8,128)S(1)} %get-tuple-element.25), channel_id=1, source_target_pairs={{0,3},{1,0},{2,1},{3,2},{4,7},{5,4},{6,5},{7,6},{8,11},{9,8},{10,9... | collective-permute-start | bytes 24584 | tf_op jit(solution)/shard_map/ppermute | solution.py:11
  43.6 13.2 %collective-permute-start.2 = (f32[128,16]{0,1:T(8,128)S(1)}, f32[128,16]{0,1:T(8,128)}, u32[]{:S(2)}, u32[]{:S(2)}) collective-permute-start(f32[128,16]{0,1:T(8,128)S(1)} %get-tuple-element.24), channel_id=1, source_target_pairs={{0,1},{1,2},{2,3},{3,0},{4,5},{5,6},{6,7},{7,4},{8,9},{9,10},{10,1... | collective-permute-start | bytes 24584 | tf_op jit(solution)/shard_map/ppermute | solution.py:11
  43.6 14.5 %collective-permute-start.3 = (f32[128,16]{0,1:T(8,128)S(1)}, f32[128,16]{0,1:T(8,128)}, u32[]{:S(2)}, u32[]{:S(2)}) collective-permute-start(f32[128,16]{0,1:T(8,128)S(1)} %get-tuple-element.23), channel_id=1, source_target_pairs={{0,3},{1,0},{2,1},{3,2},{4,7},{5,4},{6,5},{7,6},{8,11},{9,8},{10,9... | collective-permute-start | bytes 24584 | tf_op jit(solution)/shard_map/ppermute | solution.py:11
  47.4 12.0 %collective-permute-start.4 = (f32[128,16]{0,1:T(8,128)S(1)}, f32[128,16]{0,1:T(8,128)}, u32[]{:S(2)}, u32[]{:S(2)}) collective-permute-start(f32[128,16]{0,1:T(8,128)S(1)} %get-tuple-element.22), channel_id=1, source_target_pairs={{0,4},{4,8},{8,12},{12,16},{16,20},{20,24},{24,28},{28,0},{1,5},{5... | collective-permute-start | bytes 24584 | tf_op jit(solution)/shard_map/ppermute | solution.py:11
  48.2 2.2 %copy-start.11 = (s32[80]{0:T(128)S(1)}, s32[80]{0:T(128)}, u32[]{:S(2)}) copy-start(s32[80]{0:T(128)} %slice_bitcast_fusion.18) | copy-start | bytes 964
  51.5 18.8 %copy-start.8 = (s32[1,1,6]{2,1,0:T(1,128)S(1)}, s32[1,1,6]{2,1,0:T(1,128)}, u32[]{:S(2)}) copy-start(s32[1,1,6]{2,1,0:T(1,128)} %param.19) | copy-start | bytes 76
  51.5 9.1 %collective-permute-start.5 = (f32[128,16]{0,1:T(8,128)S(1)}, f32[128,16]{0,1:T(8,128)S(1)}, u32[]{:S(2)}, u32[]{:S(2)}) collective-permute-start(f32[128,16]{0,1:T(8,128)S(1)} %get-tuple-element.21), channel_id=1, source_target_pairs={{0,28},{4,0},{8,4},{12,8},{16,12},{20,16},{24,20},{28,24},{1,29},{... | collective-permute-start | bytes 24584 | tf_op jit(solution)/shard_map/ppermute | solution.py:11
  84.2 2.9 %copy-start.10 = (pred[6]{0:T(512)(128)(4,1)S(1)}, pred[6]{0:T(512)(128)(4,1)}, u32[]{:S(2)}) copy-start(pred[6]{0:T(512)(128)(4,1)} %copy-done.9) | copy-start | bytes 22
  84.2 3.1 %copy-start.12 = (s32[80]{0:T(128)S(1)}, s32[80]{0:T(128)}, u32[]{:S(2)}) copy-start(s32[80]{0:T(128)} %slice_bitcast_fusion.18) | copy-start | bytes 964
  87.2 9.9 %collective-permute-start.6 = (f32[128,16]{0,1:T(8,128)S(1)}, f32[128,16]{0,1:T(8,128)S(1)}, u32[]{:S(2)}, u32[]{:S(2)}) collective-permute-start(f32[128,16]{0,1:T(8,128)S(1)} %get-tuple-element.20), channel_id=1, source_target_pairs={{0,1},{1,2},{2,3},{3,0},{4,5},{5,6},{6,7},{7,4},{8,9},{9,10},{10,1... | collective-permute-start | bytes 24584 | tf_op jit(solution)/shard_map/ppermute | solution.py:11
  89.5 10.3 %collective-permute-start.7 = (f32[128,16]{0,1:T(8,128)S(1)}, f32[128,16]{0,1:T(8,128)S(1)}, u32[]{:S(2)}, u32[]{:S(2)}) collective-permute-start(f32[128,16]{0,1:T(8,128)S(1)} %get-tuple-element.19), channel_id=1, source_target_pairs={{0,3},{1,0},{2,1},{3,2},{4,7},{5,4},{6,5},{7,6},{8,11},{9,8},{10,9... | collective-permute-start | bytes 24584 | tf_op jit(solution)/shard_map/ppermute | solution.py:11
  93.3 6.5 %collective-permute-start.8 = (f32[128,16]{0,1:T(8,128)S(1)}, f32[128,16]{0,1:T(8,128)S(1)}, u32[]{:S(2)}, u32[]{:S(2)}) collective-permute-start(f32[128,16]{0,1:T(8,128)S(1)} %get-tuple-element.18), channel_id=1, source_target_pairs={{0,1},{1,2},{2,3},{3,0},{4,5},{5,6},{6,7},{7,4},{8,9},{9,10},{10,1... | collective-permute-start | bytes 24584 | tf_op jit(solution)/shard_map/ppermute | solution.py:11
  93.3 6.5 %collective-permute-start.9 = (f32[128,16]{0,1:T(8,128)S(1)}, f32[128,16]{0,1:T(8,128)S(1)}, u32[]{:S(2)}, u32[]{:S(2)}) collective-permute-start(f32[128,16]{0,1:T(8,128)S(1)} %get-tuple-element.17), channel_id=1, source_target_pairs={{0,3},{1,0},{2,1},{3,2},{4,7},{5,4},{6,5},{7,6},{8,11},{9,8},{10,9... | collective-permute-start | bytes 24584 | tf_op jit(solution)/shard_map/ppermute | solution.py:11
  97.1 4.0 %collective-permute-start.10 = (f32[128,16]{0,1:T(8,128)S(1)}, f32[128,16]{0,1:T(8,128)S(1)}, u32[]{:S(2)}, u32[]{:S(2)}) collective-permute-start(f32[128,16]{0,1:T(8,128)S(1)} %get-tuple-element.16), channel_id=1, source_target_pairs={{0,4},{4,8},{8,12},{12,16},{16,20},{20,24},{24,28},{28,0},{1,5},{5... | collective-permute-start | bytes 24584 | tf_op jit(solution)/shard_map/ppermute | solution.py:11
  97.1 4.0 %collective-permute-start.11 = (f32[128,16]{0,1:T(8,128)S(1)}, f32[128,16]{0,1:T(8,128)S(1)}, u32[]{:S(2)}, u32[]{:S(2)}) collective-permute-start(f32[128,16]{0,1:T(8,128)S(1)} %get-tuple-element.15), channel_id=1, source_target_pairs={{0,28},{4,0},{8,4},{12,8},{16,12},{20,16},{24,20},{28,24},{1,29},{... | collective-permute-start | bytes 24584 | tf_op jit(solution)/shard_map/ppermute | solution.py:11
  101.3 20.4 %copy-start.4 = (f32[1280,16]{0,1:T(8,128)S(1)}, f32[1280,16]{0,1:T(8,128)}, u32[]{:S(2)}) copy-start(f32[1280,16]{0,1:T(8,128)} %copy-done.3) | copy-start | bytes 245764
  126.4 9.3 %collective-permute-start.12 = (f32[128,16]{0,1:T(8,128)S(1)}, f32[128,16]{0,1:T(8,128)S(1)}, u32[]{:S(2)}, u32[]{:S(2)}) collective-permute-start(f32[128,16]{0,1:T(8,128)S(1)} %get-tuple-element.14), channel_id=1, source_target_pairs={{0,1},{1,2},{2,3},{3,0},{4,5},{5,6},{6,7},{7,4},{8,9},{9,10},{10,1... | collective-permute-start | bytes 24584 | tf_op jit(solution)/shard_map/ppermute | solution.py:11
  128.0 10.3 %collective-permute-start.13 = (f32[128,16]{0,1:T(8,128)S(1)}, f32[128,16]{0,1:T(8,128)S(1)}, u32[]{:S(2)}, u32[]{:S(2)}) collective-permute-start(f32[128,16]{0,1:T(8,128)S(1)} %get-tuple-element.13), channel_id=1, source_target_pairs={{0,3},{1,0},{2,1},{3,2},{4,7},{5,4},{6,5},{7,6},{8,11},{9,8},{10,9... | collective-permute-start | bytes 24584 | tf_op jit(solution)/shard_map/ppermute | solution.py:11
  131.9 6.5 %collective-permute-start.14 = (f32[128,16]{0,1:T(8,128)S(1)}, f32[128,16]{0,1:T(8,128)S(1)}, u32[]{:S(2)}, u32[]{:S(2)}) collective-permute-start(f32[128,16]{0,1:T(8,128)S(1)} %get-tuple-element.12), channel_id=1, source_target_pairs={{0,1},{1,2},{2,3},{3,0},{4,5},{5,6},{6,7},{7,4},{8,9},{9,10},{10,1... | collective-permute-start | bytes 24584 | tf_op jit(solution)/shard_map/ppermute | solution.py:11
  131.9 6.5 %collective-permute-start.15 = (f32[128,16]{0,1:T(8,128)S(1)}, f32[128,16]{0,1:T(8,128)S(1)}, u32[]{:S(2)}, u32[]{:S(2)}) collective-permute-start(f32[128,16]{0,1:T(8,128)S(1)} %get-tuple-element.11), channel_id=1, source_target_pairs={{0,3},{1,0},{2,1},{3,2},{4,7},{5,4},{6,5},{7,6},{8,11},{9,8},{10,9... | collective-permute-start | bytes 24584 | tf_op jit(solution)/shard_map/ppermute | solution.py:11
  135.7 4.0 %collective-permute-start.16 = (f32[128,16]{0,1:T(8,128)S(1)}, f32[128,16]{0,1:T(8,128)S(1)}, u32[]{:S(2)}, u32[]{:S(2)}) collective-permute-start(f32[128,16]{0,1:T(8,128)S(1)} %get-tuple-element.10), channel_id=1, source_target_pairs={{0,4},{4,8},{8,12},{12,16},{16,20},{20,24},{24,28},{28,0},{1,5},{5... | collective-permute-start | bytes 24584 | tf_op jit(solution)/shard_map/ppermute | solution.py:11
  135.7 4.0 %collective-permute-start.17 = (f32[128,16]{0,1:T(8,128)S(1)}, f32[128,16]{0,1:T(8,128)S(1)}, u32[]{:S(2)}, u32[]{:S(2)}) collective-permute-start(f32[128,16]{0,1:T(8,128)S(1)} %get-tuple-element.9), channel_id=1, source_target_pairs={{0,28},{4,0},{8,4},{12,8},{16,12},{20,16},{24,20},{28,24},{1,29},{... | collective-permute-start | bytes 24584 | tf_op jit(solution)/shard_map/ppermute | solution.py:11
  (2 other events, 1.6 us)
where the time goes:
time: 150 us; the launch traced here: 149 us
  local copies, waits for them, and re-layouts  48.4 us (32%)
  blocking collectives  38.5 us (26%)
  starting transfers between devices  34.5 us (23%)
  matrix products  20.4 us (14%)
  other arithmetic  3.46 us (2%)
  waiting for transfers between devices  2.68 us (2%)
    ppermute x18, starting transfers between devices, from_behind(): lax.ppermute(shard, axis, [(i, (i + by) % peers) for i in range(peers)])  31.1 us
    all_gather x3, blocking collectives, body(): lax.all_gather(local_coarse, 'sub', axis=0, tiled=True)  27.8 us
    gather x6, local copies, waits for them, and re-layouts, body(): permuted = jnp.take_along_axis(received, matched[:, :, None], axis=1)  24.4 us
    all_gather x1, blocking collectives, body(): every_ids = lax.all_gather(own_map, 'sub', axis=0, tiled=True)  10.7 us
    unnamed x47, local copies, waits for them, and re-layouts  8.21 us
    dot_general x3, matrix products, body(): jnp.einsum('tij,tjr->tir', tile_block, picked, preferred_element_type=jnp...  6.87 us
    gather x2, local copies, waits for them, and re-layouts, body(): jnp.take(inverse_rows, every_ids, axis=1)  5.21 us
    dot_general x3, matrix products, body(): jnp.einsum('bt,tir->bir', row_table, products, precision=lax.Precision.HI...  4.98 us
  transfers between devices with their start and end apart: 19, of which 2 were waited for; matrix products, arithmetic and copies ran while one was open for 11% of the time, Pallas kernels for 0%

commit v1 on v0

--- a/solution.py
+++ b/solution.py
@@ -41,7 +41,14 @@
     row_table = (listing[:, 0][None, :] == block_ids[:, None]).astype(jnp.float32)
     face_table = (faces_here[None, :] == block_ids[:, None]).astype(jnp.float32)
     stride = max(lax.axis_size("reg") // 4, 1)
-    every_ids = lax.all_gather(own_map, "sub", axis=0, tiled=True)
+    ways, here = (lax.axis_size("sub"), lax.axis_index("sub"))
+    every_ids, reach = (own_map, 1)
+    while reach < ways:
+        theirs = lax.ppermute(every_ids, "sub", [(d, d ^ reach) for d in range(ways)])
+        mine_first = jnp.concatenate([every_ids, theirs], axis=0)
+        theirs_first = jnp.concatenate([theirs, every_ids], axis=0)
+        every_ids = jnp.where(here & reach == 0, mine_first, theirs_first)
+        reach = 2 * reach
     outgoing_part = jnp.take(inverse_rows, every_ids, axis=1).reshape(
         held_rows, lax.axis_size("sub"), own_count
     )

time: 150 us -> 149 us (level)
  blocking collectives: 38.5 us -> 27.9 us
  starting transfers between devices: 34.5 us -> 40.2 us
  local copies, waits for them, and re-layouts: 48.4 us -> 44.1 us
  other arithmetic: 3.46 us -> 6.98 us
  matrix products: 20.4 us -> 23 us
  waiting for transfers between devices: 2.68 us -> 4.38 us
    all_gather x1 -> x0, blocking collectives: 10.7 us -> none  [body(): every_ids = lax.all_gather(own_map, 'sub', axis=0, tiled=True)]
    ppermute x0 -> x3, starting transfers between devices: none -> 5.08 us  [body(): lax.ppermute(every_ids, 'sub', [(d, d ^ reach) for d in range(ways)])]
    gather x6, local copies, waits for them, and re-layouts: 24.4 us -> 21.6 us  [body(): permuted = jnp.take_along_axis(received, matched[:, :, None], axis=1)]
    gather x2, local copies, waits for them, and re-layouts: 5.21 us -> 2.99 us  [body(): jnp.take(inverse_rows, every_ids, axis=1)]
    ppermute x0 -> x3, waiting for transfers between devices: none -> 1.7 us  [body(): lax.ppermute(every_ids, 'sub', [(d, d ^ reach) for d in range(ways)])]
    unnamed x47 -> x43, local copies, waits for them, and re-layouts: 8.21 us -> 8.19 us
  transfers between devices with their start and end apart: 19 -> 22, of which waited for: 2 -> 3; matrix products, arithmetic and copies ran while one was open for 11% -> 15% of each run, Pallas kernels for 0% -> 0%
where the time goes in v1:
time: 149 us; the launch traced here: 148 us
  local copies, waits for them, and re-layouts  44.1 us (30%)
  starting transfers between devices  40.2 us (27%)
  blocking collectives  27.9 us (19%)
  matrix products  23 us (15%)
  other arithmetic  6.98 us (5%)
  waiting for transfers between devices  4.38 us (3%)
    ppermute x18, starting transfers between devices, from_behind(): lax.ppermute(shard, axis, [(i, (i + by) % peers) for i in range(peers)])  31 us
    all_gather x3, blocking collectives, body(): lax.all_gather(local_coarse, 'sub', axis=0, tiled=True)  27.9 us
    gather x6, local copies, waits for them, and re-layouts, body(): permuted = jnp.take_along_axis(received, matched[:, :, None], axis=1)  21.6 us
    unnamed x43, local copies, waits for them, and re-layouts  8.19 us
    dot_general x3, matrix products, body(): jnp.einsum('tij,tjr->tir', tile_block, picked, preferred_element_type=jnp...  6.9 us
    dot_general x3, matrix products, body(): jnp.einsum('bt,tir->bir', row_table, products, precision=lax.Precision.HI...  5.62 us
    ppermute x3, starting transfers between devices, body(): lax.ppermute(every_ids, 'sub', [(d, d ^ reach) for d in range(ways)])  5.08 us
    dot_general x3, matrix products, body(): jnp.dot(own_block, lax.all_gather(local_coarse, 'sub', axis=0, tiled=True...  4.59 us
  transfers between devices with their start and end apart: 22, of which 3 were waited for; matrix products, arithmetic and copies ran while one was open for 15% of the time, Pallas kernels for 0%

profile of v1, /device:TPU:0, one launch (start us, length us, event | category | flops | bytes accessed | tf_op | source)
XLA Modules:
  0.0 147.6 jit_solution(11925497378523238673)
XLA Ops:
  7.7 2.6 %collective-permute-start.1 = (s32[256]{0:T(256)S(1)}, s32[256]{0:T(256)S(1)}, u32[]{:S(2)}, u32[]{:S(2)}) collective-permute-start(s32[256]{0:T(256)S(1)} %add_select_fusion.4), channel_id=1, source_target_pairs={{0,8},{4,12},{8,0},{12,4},{16,24},{20,28},{24,16},{28,20},{1,9},{5... | collective-permute-start | bytes 3080 | tf_op jit(solution)/shard_map/ppermute | solution.py:47
  11.9 1.9 %collective-permute-start.2 = (s32[512]{0:T(512)S(1)}, s32[512]{0:T(512)S(1)}, u32[]{:S(2)}, u32[]{:S(2)}) collective-permute-start(s32[512]{0:T(512)S(1)} %add_select_fusion.2), channel_id=1, source_target_pairs={{0,16},{4,20},{8,24},{12,28},{16,0},{20,4},{24,8},{28,12},{1,17},{... | collective-permute-start | bytes 6152 | tf_op jit(solution)/shard_map/ppermute | solution.py:47
  13.9 1.7 %collective-permute-done.2 = s32[512]{0:T(512)S(1)} collective-permute-done((s32[512]{0:T(512)S(1)}, s32[512]{0:T(512)S(1)}, u32[]{:S(2)}, u32[]{:S(2)}) %collective-permute-start.2) | collective-permute-done | bytes 2080 | tf_op jit(solution)/shard_map/ppermute | solution.py:47
  15.6 2.8 %gather_fusion = f32[1024,64]{1,0:T(8,128)S(1)} fusion(f32[64,512]{0,1:T(8,128)S(1)} %bitcast.255, s32[1024]{0:T(1024)S(1)} %broadcast_clamp_fusion), kind=kCustom, calls=%fused_computation.9 | custom fusion | bytes 528384 | tf_op jit(solution)/shard_map/jit(_take)/gather | solution.py:52
  19.3 4.1 %all-to-all-start = ((f32[64,8,128]{2,0,1:T(8,128)}), f32[64,8,128]{2,0,1:T(8,128)S(1)}, u32[]{:S(2)}, u32[]{:S(2)}) async-start(f32[64,8,128]{2,0,1:T(8,128)} %broadcast_select_fusion), calls=%async_computation | async-start | bytes 524288 | tf_op jit(solution)/shard_map/all_to_all | solution.py:55
  23.4 10.3 %all_gather.9 = f32[1024,16]{0,1:T(8,128)S(1)} all-gather(f32[128,16]{0,1:T(8,128)S(1)} %fusion.37), channel_id=1, replica_groups=mesh['sub'=8,'reg'=4] {'sub'}, dimensions={0}, use_global_device_ids=true | all-gather | bytes 73728 | tf_op jit(solution)/shard_map/all_gather | solution.py:65
  33.8 4.0 %gather_fusion.1 = f32[1024,128]{1,0:T(8,128)} fusion(f32[512,128]{1,0:T(8,128)S(1)} %bitcast.254, s32[1024]{0:T(1024)S(1)} %broadcast_clamp_fusion), kind=kCustom, calls=%fused_computation.10 | custom fusion | bytes 1052672 | tf_op jit(solution)/shard_map/jit(_take)/gather | solution.py:57
  37.8 1.5 %convolution_convert_fusion.2 = bf16[128,16]{0,1:T(8,128)(2,1)S(1)} fusion(f32[1024,16]{0,1:T(8,128)S(1)} %all_gather.9, f32[1024,128]{1,0:T(8,128)} %gather_fusion.1, pred[1024]{0:T(1024)(128)(4,1)S(1)} %compare_and_fusion.2), kind=kOutput, calls=%fused_computation.38 | convolution fusion | flops 25298944 | bytes 594944 | tf_op jit(solution)/shard_map/dot_general | solution.py:63
  40.3 1.6 %collective-permute-start.3 = (f32[128,16]{0,1:T(8,128)S(1)}, f32[128,16]{0,1:T(8,128)}, u32[]{:S(2)}, u32[]{:S(2)}) collective-permute-start(f32[128,16]{0,1:T(8,128)S(1)} %get-tuple-element.26), channel_id=1, source_target_pairs={{0,1},{1,2},{2,3},{3,0},{4,5},{5,6},{6,7},{7,4},{8,9},{9,10},{10,1... | collective-permute-start | bytes 24584 | tf_op jit(solution)/shard_map/ppermute | solution.py:11
  41.9 2.2 %collective-permute-start.4 = (f32[128,16]{0,1:T(8,128)S(1)}, f32[128,16]{0,1:T(8,128)}, u32[]{:S(2)}, u32[]{:S(2)}) collective-permute-start(f32[128,16]{0,1:T(8,128)S(1)} %get-tuple-element.25), channel_id=1, source_target_pairs={{0,3},{1,0},{2,1},{3,2},{4,7},{5,4},{6,5},{7,6},{8,11},{9,8},{10,9... | collective-permute-start | bytes 24584 | tf_op jit(solution)/shard_map/ppermute | solution.py:11
  44.1 3.8 %collective-permute-start.6 = (f32[128,16]{0,1:T(8,128)S(1)}, f32[128,16]{0,1:T(8,128)}, u32[]{:S(2)}, u32[]{:S(2)}) collective-permute-start(f32[128,16]{0,1:T(8,128)S(1)} %get-tuple-element.23), channel_id=1, source_target_pairs={{0,3},{1,0},{2,1},{3,2},{4,7},{5,4},{6,5},{7,6},{8,11},{9,8},{10,9... | collective-permute-start | bytes 24584 | tf_op jit(solution)/shard_map/ppermute | solution.py:11
  48.8 2.2 %fusion.11 = f32[80,128,16]{1,2,0:T(8,128)S(1)} fusion(bf16[1,1,80,128,128]{4,3,2,1,0:T(8,128)(2,1)S(1)} %copy-done, bf16[80,128,16]{1,2,0:T(8,128)(2,1)S(1)} %gather_fusion.2, pred[80]{0:T(512)(128)(4,1)} %get-tuple-element.4), kind=kOutput, calls=%fused_computation.25 | convolution fusion | flops 42106880 | bytes 3604560 | tf_op jit(solution)/shard_map/tij,tjr->tir/dot_general | solution.py:74
  52.1 2.6 %collective-permute-start.8 = (f32[128,16]{0,1:T(8,128)S(1)}, f32[128,16]{0,1:T(8,128)S(1)}, u32[]{:S(2)}, u32[]{:S(2)}) collective-permute-start(f32[128,16]{0,1:T(8,128)S(1)} %get-tuple-element.21), channel_id=1, source_target_pairs={{0,28},{4,0},{8,4},{12,8},{16,12},{20,16},{24,20},{28,24},{1,29},{... | collective-permute-start | bytes 24584 | tf_op jit(solution)/shard_map/ppermute | solution.py:11
  54.7 1.3 constant_dynamic-update-slice_fusion.5
  58.6 1.3 constant_dynamic-update-slice_fusion.2
  62.8 7.0 %gather_fusion.4 = f32[768,16]{1,0:T(8,128)} fusion(f32[6,128,16]{2,1,0:T(8,128)S(1)} %copy.35, s32[768]{0:T(1024)S(1)} %bitcast.250), kind=kCustom, calls=%fused_computation.2.clone | custom fusion | bytes 104448 | tf_op jit(solution)/shard_map/jit(take_along_axis)/gather | solution.py:86
  72.4 8.4 %all_gather.10 = f32[1024,16]{0,1:T(8,128)S(1)} all-gather(f32[128,16]{0,1:T(8,128)S(1)} %convolution_bitcast_fusion.4), channel_id=1, replica_groups=mesh['sub'=8,'reg'=4] {'sub'}, dimensions={0}, use_global_device_ids=true | all-gather | bytes 73728 | tf_op jit(solution)/shard_map/all_gather | solution.py:65
  80.7 1.5 %convolution_convert_fusion.1 = bf16[128,16]{0,1:T(8,128)(2,1)S(1)} fusion(f32[1024,16]{0,1:T(8,128)S(1)} %all_gather.10, f32[1024,128]{1,0:T(8,128)} %gather_fusion.1, pred[1024]{0:T(1024)(128)(4,1)S(1)} %compare_and_fusion.2), kind=kOutput, calls=%fused_computation.37 | convolution fusion | flops 25298944 | bytes 594944 | tf_op jit(solution)/shard_map/dot_general | solution.py:63
  84.1 2.4 %fusion.14 = f32[80,128,16]{1,2,0:T(8,128)} fusion(bf16[1,1,80,128,128]{4,3,2,1,0:T(8,128)(2,1)S(1)} %copy-done, bf16[80,128,16]{1,2,0:T(8,128)(2,1)S(1)} %gather_fusion.5, pred[80]{0:T(512)(128)(4,1)S(1)} %copy-done.12), kind=kOutput, calls=%fused_computation.26 | convolution fusion | flops 42106880 | bytes 3604560 | tf_op jit(solution)/shard_map/tij,tjr->tir/dot_general | solution.py:74
  87.2 2.2 %fusion.25 = f32[10,128,16]{1,0,2:T(8,128)} fusion(f32[80,128,16]{1,2,0:T(8,128)} %fusion.14, s32[80]{0:T(128)S(1)} %copy-done.11), kind=kOutput, calls=%fused_computation.41 | convolution fusion | flops 19661600 | bytes 737600 | tf_op jit(solution)/shard_map/bt,tir->bir/dot_general | solution.py:77
  89.4 3.8 %collective-permute-start.10 = (f32[128,16]{0,1:T(8,128)S(1)}, f32[128,16]{0,1:T(8,128)S(1)}, u32[]{:S(2)}, u32[]{:S(2)}) collective-permute-start(f32[128,16]{0,1:T(8,128)S(1)} %get-tuple-element.19), channel_id=1, source_target_pairs={{0,3},{1,0},{2,1},{3,2},{4,7},{5,4},{6,5},{7,6},{8,11},{9,8},{10,9... | collective-permute-start | bytes 24584 | tf_op jit(solution)/shard_map/ppermute | solution.py:11
  93.2 3.8 %collective-permute-start.12 = (f32[128,16]{0,1:T(8,128)S(1)}, f32[128,16]{0,1:T(8,128)S(1)}, u32[]{:S(2)}, u32[]{:S(2)}) collective-permute-start(f32[128,16]{0,1:T(8,128)S(1)} %get-tuple-element.17), channel_id=1, source_target_pairs={{0,3},{1,0},{2,1},{3,2},{4,7},{5,4},{6,5},{7,6},{8,11},{9,8},{10,9... | collective-permute-start | bytes 24584 | tf_op jit(solution)/shard_map/ppermute | solution.py:11
  97.0 2.6 %collective-permute-start.14 = (f32[128,16]{0,1:T(8,128)S(1)}, f32[128,16]{0,1:T(8,128)S(1)}, u32[]{:S(2)}, u32[]{:S(2)}) collective-permute-start(f32[128,16]{0,1:T(8,128)S(1)} %get-tuple-element.15), channel_id=1, source_target_pairs={{0,28},{4,0},{8,4},{12,8},{16,12},{20,16},{24,20},{28,24},{1,29},{... | collective-permute-start | bytes 24584 | tf_op jit(solution)/shard_map/ppermute | solution.py:11
  101.2 7.0 %gather_fusion.7 = f32[768,16]{1,0:T(8,128)} fusion(f32[6,128,16]{2,1,0:T(8,128)S(1)} %copy.40, s32[768]{0:T(1024)S(1)} %bitcast.251), kind=kCustom, calls=%fused_computation.7.clone | custom fusion | bytes 104448 | tf_op jit(solution)/shard_map/jit(take_along_axis)/gather | solution.py:86
  110.8 9.3 %all_gather.11 = f32[1024,16]{0,1:T(8,128)S(1)} all-gather(f32[128,16]{0,1:T(8,128)S(1)} %convolution_bitcast_fusion.3), channel_id=1, replica_groups=mesh['sub'=8,'reg'=4] {'sub'}, dimensions={0}, use_global_device_ids=true | all-gather | bytes 73728 | tf_op jit(solution)/shard_map/all_gather | solution.py:65
  120.1 1.5 %convolution_convert_fusion = bf16[128,16]{0,1:T(8,128)(2,1)S(1)} fusion(f32[1024,16]{0,1:T(8,128)S(1)} %all_gather.11, f32[1024,128]{1,0:T(8,128)} %gather_fusion.1, pred[1024]{0:T(1024)(128)(4,1)S(1)} %compare_and_fusion.2), kind=kOutput, calls=%fused_computation.36 | convolution fusion | flops 25298944 | bytes 594944 | tf_op jit(solution)/shard_map/dot_general | solution.py:63
  123.3 2.4 %fusion.17 = f32[80,128,16]{1,2,0:T(8,128)} fusion(bf16[1,1,80,128,128]{4,3,2,1,0:T(8,128)(2,1)S(1)} %copy-done, bf16[80,128,16]{1,2,0:T(8,128)(2,1)S(1)} %gather_fusion.8, pred[80]{0:T(512)(128)(4,1)S(1)} %copy-done.12), kind=kOutput, calls=%fused_computation.27 | convolution fusion | flops 42106880 | bytes 3604560 | tf_op jit(solution)/shard_map/tij,tjr->tir/dot_general | solution.py:74
  126.4 2.2 %fusion.23 = f32[10,128,16]{1,0,2:T(8,128)} fusion(f32[80,128,16]{1,2,0:T(8,128)} %fusion.17, s32[80]{0:T(128)S(1)} %copy-done.11), kind=kOutput, calls=%fused_computation.39 | convolution fusion | flops 19661600 | bytes 737600 | tf_op jit(solution)/shard_map/bt,tir->bir/dot_general | solution.py:77
  128.6 3.8 %collective-permute-start.16 = (f32[128,16]{0,1:T(8,128)S(1)}, f32[128,16]{0,1:T(8,128)S(1)}, u32[]{:S(2)}, u32[]{:S(2)}) collective-permute-start(f32[128,16]{0,1:T(8,128)S(1)} %get-tuple-element.13), channel_id=1, source_target_pairs={{0,3},{1,0},{2,1},{3,2},{4,7},{5,4},{6,5},{7,6},{8,11},{9,8},{10,9... | collective-permute-start | bytes 24584 | tf_op jit(solution)/shard_map/ppermute | solution.py:11
  132.4 3.8 %collective-permute-start.18 = (f32[128,16]{0,1:T(8,128)S(1)}, f32[128,16]{0,1:T(8,128)S(1)}, u32[]{:S(2)}, u32[]{:S(2)}) collective-permute-start(f32[128,16]{0,1:T(8,128)S(1)} %get-tuple-element.11), channel_id=1, source_target_pairs={{0,3},{1,0},{2,1},{3,2},{4,7},{5,4},{6,5},{7,6},{8,11},{9,8},{10,9... | collective-permute-start | bytes 24584 | tf_op jit(solution)/shard_map/ppermute | solution.py:11
  136.2 2.6 %collective-permute-start.20 = (f32[128,16]{0,1:T(8,128)S(1)}, f32[128,16]{0,1:T(8,128)S(1)}, u32[]{:S(2)}, u32[]{:S(2)}) collective-permute-start(f32[128,16]{0,1:T(8,128)S(1)} %get-tuple-element.9), channel_id=1, source_target_pairs={{0,28},{4,0},{8,4},{12,8},{16,12},{20,16},{24,20},{28,24},{1,29},{... | collective-permute-start | bytes 24584 | tf_op jit(solution)/shard_map/ppermute | solution.py:11
  140.4 5.1 %gather_fusion.10 = f32[768,16]{1,0:T(8,128)S(1)} fusion(f32[6,128,16]{2,1,0:T(8,128)S(1)} %copy.45, s32[768]{0:T(1024)S(1)} %bitcast.252), kind=kCustom, calls=%fused_computation.8.clone | custom fusion | bytes 104448 | tf_op jit(solution)/shard_map/jit(take_along_axis)/gather | solution.py:86
  (130 shorter events, 33.0 us)
Async XLA Ops:
  0.6 48.1 %copy-start = (bf16[1,1,80,128,128]{4,3,2,1,0:T(8,128)(2,1)S(1)}, bf16[1,1,80,128,128]{4,3,2,1,0:T(8,128)(2,1)}, u32[]{:S(2)}) copy-start(bf16[1,1,80,128,128]{4,3,2,1,0:T(8,128)(2,1)} %param.16) | copy-start | bytes 7864324
  0.6 33.0 %copy-start.5 = (s32[1,1,6,128]{3,1,2,0:T(1,128)S(1)}, s32[1,1,6,128]{3,1,2,0:T(1,128)}, u32[]{:S(2)}) copy-start(s32[1,1,6,128]{3,1,2,0:T(1,128)} %param.20) | copy-start | bytes 9220
  0.7 33.0 %copy-start.6 = (f32[1,1,1280]{2,1,0:T(1,128)S(1)}, f32[1,1,1280]{2,1,0:T(1,128)}, u32[]{:S(2)}) copy-start(f32[1,1,1280]{2,1,0:T(1,128)} %param.18) | copy-start | bytes 15364
  0.7 6.3 %collective-permute-start = (s32[128]{0:T(128)}, s32[128]{0:T(128)S(1)}, u32[]{:S(2)}, u32[]{:S(2)}) collective-permute-start(s32[128]{0:T(128)} %bitcast.274), channel_id=1, source_target_pairs={{0,4},{4,0},{8,12},{12,8},{16,20},{20,16},{24,28},{28,24},{1,5},{5... | collective-permute-start | bytes 1544 | tf_op jit(solution)/shard_map/ppermute | solution.py:47
  5.0 35.1 %copy-start.8 = (pred[6]{0:T(512)(128)(4,1)}, pred[6]{0:T(512)(128)(4,1)S(1)}, u32[]{:S(2)}) copy-start(pred[6]{0:T(512)(128)(4,1)S(1)} %compare_and_fusion.3) | copy-start | bytes 22
  7.7 4.2 %collective-permute-start.1 = (s32[256]{0:T(256)S(1)}, s32[256]{0:T(256)S(1)}, u32[]{:S(2)}, u32[]{:S(2)}) collective-permute-start(s32[256]{0:T(256)S(1)} %add_select_fusion.4), channel_id=1, source_target_pairs={{0,8},{4,12},{8,0},{12,4},{16,24},{20,28},{24,16},{28,20},{1,9},{5... | collective-permute-start | bytes 3080 | tf_op jit(solution)/shard_map/ppermute | solution.py:47
  11.9 3.7 %collective-permute-start.2 = (s32[512]{0:T(512)S(1)}, s32[512]{0:T(512)S(1)}, u32[]{:S(2)}, u32[]{:S(2)}) collective-permute-start(s32[512]{0:T(512)S(1)} %add_select_fusion.2), channel_id=1, source_target_pairs={{0,16},{4,20},{8,24},{12,28},{16,0},{20,4},{24,8},{28,12},{1,17},{... | collective-permute-start | bytes 6152 | tf_op jit(solution)/shard_map/ppermute | solution.py:47
  19.3 14.4 %all-to-all-start = ((f32[64,8,128]{2,0,1:T(8,128)}), f32[64,8,128]{2,0,1:T(8,128)S(1)}, u32[]{:S(2)}, u32[]{:S(2)}) async-start(f32[64,8,128]{2,0,1:T(8,128)} %broadcast_select_fusion), calls=%async_computation | async-start | bytes 524288 | tf_op jit(solution)/shard_map/all_to_all | solution.py:55
  33.8 5.6 %copy-start.1 = (bf16[1,1,1280,128]{3,2,1,0:T(8,128)(2,1)S(1)}, bf16[1,1,1280,128]{3,2,1,0:T(8,128)(2,1)}, u32[]{:S(2)}) copy-start(bf16[1,1,1280,128]{3,2,1,0:T(8,128)(2,1)} %param.21) | copy-start | bytes 983044
  33.8 5.6 %copy-start.2 = (f32[1,1,1280,16]{2,3,1,0:T(8,128)S(1)}, f32[1,1,1280,16]{2,3,1,0:T(8,128)}, u32[]{:S(2)}) copy-start(f32[1,1,1280,16]{2,3,1,0:T(8,128)} %param.15) | copy-start | bytes 245764
  40.3 11.8 %collective-permute-start.3 = (f32[128,16]{0,1:T(8,128)S(1)}, f32[128,16]{0,1:T(8,128)}, u32[]{:S(2)}, u32[]{:S(2)}) collective-permute-start(f32[128,16]{0,1:T(8,128)S(1)} %get-tuple-element.26), channel_id=1, source_target_pairs={{0,1},{1,2},{2,3},{3,0},{4,5},{5,6},{6,7},{7,4},{8,9},{9,10},{10,1... | collective-permute-start | bytes 24584 | tf_op jit(solution)/shard_map/ppermute | solution.py:11
  41.9 14.2 %collective-permute-start.4 = (f32[128,16]{0,1:T(8,128)S(1)}, f32[128,16]{0,1:T(8,128)}, u32[]{:S(2)}, u32[]{:S(2)}) collective-permute-start(f32[128,16]{0,1:T(8,128)S(1)} %get-tuple-element.25), channel_id=1, source_target_pairs={{0,3},{1,0},{2,1},{3,2},{4,7},{5,4},{6,5},{7,6},{8,11},{9,8},{10,9... | collective-permute-start | bytes 24584 | tf_op jit(solution)/shard_map/ppermute | solution.py:11
  44.1 13.2 %collective-permute-start.5 = (f32[128,16]{0,1:T(8,128)S(1)}, f32[128,16]{0,1:T(8,128)}, u32[]{:S(2)}, u32[]{:S(2)}) collective-permute-start(f32[128,16]{0,1:T(8,128)S(1)} %get-tuple-element.24), channel_id=1, source_target_pairs={{0,1},{1,2},{2,3},{3,0},{4,5},{5,6},{6,7},{7,4},{8,9},{9,10},{10,1... | collective-permute-start | bytes 24584 | tf_op jit(solution)/shard_map/ppermute | solution.py:11
  44.1 14.5 %collective-permute-start.6 = (f32[128,16]{0,1:T(8,128)S(1)}, f32[128,16]{0,1:T(8,128)}, u32[]{:S(2)}, u32[]{:S(2)}) collective-permute-start(f32[128,16]{0,1:T(8,128)S(1)} %get-tuple-element.23), channel_id=1, source_target_pairs={{0,3},{1,0},{2,1},{3,2},{4,7},{5,4},{6,5},{7,6},{8,11},{9,8},{10,9... | collective-permute-start | bytes 24584 | tf_op jit(solution)/shard_map/ppermute | solution.py:11
  48.0 12.0 %collective-permute-start.7 = (f32[128,16]{0,1:T(8,128)S(1)}, f32[128,16]{0,1:T(8,128)}, u32[]{:S(2)}, u32[]{:S(2)}) collective-permute-start(f32[128,16]{0,1:T(8,128)S(1)} %get-tuple-element.22), channel_id=1, source_target_pairs={{0,4},{4,8},{8,12},{12,16},{16,20},{20,24},{24,28},{28,0},{1,5},{5... | collective-permute-start | bytes 24584 | tf_op jit(solution)/shard_map/ppermute | solution.py:11
  52.1 18.8 %copy-start.7 = (s32[1,1,6]{2,1,0:T(1,128)S(1)}, s32[1,1,6]{2,1,0:T(1,128)}, u32[]{:S(2)}) copy-start(s32[1,1,6]{2,1,0:T(1,128)} %param.19) | copy-start | bytes 76
  52.1 9.1 %collective-permute-start.8 = (f32[128,16]{0,1:T(8,128)S(1)}, f32[128,16]{0,1:T(8,128)S(1)}, u32[]{:S(2)}, u32[]{:S(2)}) collective-permute-start(f32[128,16]{0,1:T(8,128)S(1)} %get-tuple-element.21), channel_id=1, source_target_pairs={{0,28},{4,0},{8,4},{12,8},{16,12},{20,16},{24,20},{28,24},{1,29},{... | collective-permute-start | bytes 24584 | tf_op jit(solution)/shard_map/ppermute | solution.py:11
  84.1 3.0 %copy-start.9 = (pred[6]{0:T(512)(128)(4,1)S(1)}, pred[6]{0:T(512)(128)(4,1)}, u32[]{:S(2)}) copy-start(pred[6]{0:T(512)(128)(4,1)} %copy-done.8) | copy-start | bytes 22
  84.1 3.1 %copy-start.11 = (s32[80]{0:T(128)S(1)}, s32[80]{0:T(128)}, u32[]{:S(2)}) copy-start(s32[80]{0:T(128)} %slice_bitcast_fusion.18) | copy-start | bytes 964
  87.1 9.9 %collective-permute-start.9 = (f32[128,16]{0,1:T(8,128)S(1)}, f32[128,16]{0,1:T(8,128)S(1)}, u32[]{:S(2)}, u32[]{:S(2)}) collective-permute-start(f32[128,16]{0,1:T(8,128)S(1)} %get-tuple-element.20), channel_id=1, source_target_pairs={{0,1},{1,2},{2,3},{3,0},{4,5},{5,6},{6,7},{7,4},{8,9},{9,10},{10,1... | collective-permute-start | bytes 24584 | tf_op jit(solution)/shard_map/ppermute | solution.py:11
  89.4 10.3 %collective-permute-start.10 = (f32[128,16]{0,1:T(8,128)S(1)}, f32[128,16]{0,1:T(8,128)S(1)}, u32[]{:S(2)}, u32[]{:S(2)}) collective-permute-start(f32[128,16]{0,1:T(8,128)S(1)} %get-tuple-element.19), channel_id=1, source_target_pairs={{0,3},{1,0},{2,1},{3,2},{4,7},{5,4},{6,5},{7,6},{8,11},{9,8},{10,9... | collective-permute-start | bytes 24584 | tf_op jit(solution)/shard_map/ppermute | solution.py:11
  93.2 6.5 %collective-permute-start.11 = (f32[128,16]{0,1:T(8,128)S(1)}, f32[128,16]{0,1:T(8,128)S(1)}, u32[]{:S(2)}, u32[]{:S(2)}) collective-permute-start(f32[128,16]{0,1:T(8,128)S(1)} %get-tuple-element.18), channel_id=1, source_target_pairs={{0,1},{1,2},{2,3},{3,0},{4,5},{5,6},{6,7},{7,4},{8,9},{9,10},{10,1... | collective-permute-start | bytes 24584 | tf_op jit(solution)/shard_map/ppermute | solution.py:11
  93.2 6.5 %collective-permute-start.12 = (f32[128,16]{0,1:T(8,128)S(1)}, f32[128,16]{0,1:T(8,128)S(1)}, u32[]{:S(2)}, u32[]{:S(2)}) collective-permute-start(f32[128,16]{0,1:T(8,128)S(1)} %get-tuple-element.17), channel_id=1, source_target_pairs={{0,3},{1,0},{2,1},{3,2},{4,7},{5,4},{6,5},{7,6},{8,11},{9,8},{10,9... | collective-permute-start | bytes 24584 | tf_op jit(solution)/shard_map/ppermute | solution.py:11
  97.0 4.0 %collective-permute-start.13 = (f32[128,16]{0,1:T(8,128)S(1)}, f32[128,16]{0,1:T(8,128)S(1)}, u32[]{:S(2)}, u32[]{:S(2)}) collective-permute-start(f32[128,16]{0,1:T(8,128)S(1)} %get-tuple-element.16), channel_id=1, source_target_pairs={{0,4},{4,8},{8,12},{12,16},{16,20},{20,24},{24,28},{28,0},{1,5},{5... | collective-permute-start | bytes 24584 | tf_op jit(solution)/shard_map/ppermute | solution.py:11
  97.0 4.0 %collective-permute-start.14 = (f32[128,16]{0,1:T(8,128)S(1)}, f32[128,16]{0,1:T(8,128)S(1)}, u32[]{:S(2)}, u32[]{:S(2)}) collective-permute-start(f32[128,16]{0,1:T(8,128)S(1)} %get-tuple-element.15), channel_id=1, source_target_pairs={{0,28},{4,0},{8,4},{12,8},{16,12},{20,16},{24,20},{28,24},{1,29},{... | collective-permute-start | bytes 24584 | tf_op jit(solution)/shard_map/ppermute | solution.py:11
  101.2 20.4 %copy-start.4 = (f32[1280,16]{0,1:T(8,128)S(1)}, f32[1280,16]{0,1:T(8,128)}, u32[]{:S(2)}) copy-start(f32[1280,16]{0,1:T(8,128)} %copy-done.3) | copy-start | bytes 245764
  126.3 9.9 %collective-permute-start.15 = (f32[128,16]{0,1:T(8,128)S(1)}, f32[128,16]{0,1:T(8,128)S(1)}, u32[]{:S(2)}, u32[]{:S(2)}) collective-permute-start(f32[128,16]{0,1:T(8,128)S(1)} %get-tuple-element.14), channel_id=1, source_target_pairs={{0,1},{1,2},{2,3},{3,0},{4,5},{5,6},{6,7},{7,4},{8,9},{9,10},{10,1... | collective-permute-start | bytes 24584 | tf_op jit(solution)/shard_map/ppermute | solution.py:11
  128.6 10.3 %collective-permute-start.16 = (f32[128,16]{0,1:T(8,128)S(1)}, f32[128,16]{0,1:T(8,128)S(1)}, u32[]{:S(2)}, u32[]{:S(2)}) collective-permute-start(f32[128,16]{0,1:T(8,128)S(1)} %get-tuple-element.13), channel_id=1, source_target_pairs={{0,3},{1,0},{2,1},{3,2},{4,7},{5,4},{6,5},{7,6},{8,11},{9,8},{10,9... | collective-permute-start | bytes 24584 | tf_op jit(solution)/shard_map/ppermute | solution.py:11
  132.4 6.5 %collective-permute-start.17 = (f32[128,16]{0,1:T(8,128)S(1)}, f32[128,16]{0,1:T(8,128)S(1)}, u32[]{:S(2)}, u32[]{:S(2)}) collective-permute-start(f32[128,16]{0,1:T(8,128)S(1)} %get-tuple-element.12), channel_id=1, source_target_pairs={{0,1},{1,2},{2,3},{3,0},{4,5},{5,6},{6,7},{7,4},{8,9},{9,10},{10,1... | collective-permute-start | bytes 24584 | tf_op jit(solution)/shard_map/ppermute | solution.py:11
  132.4 6.5 %collective-permute-start.18 = (f32[128,16]{0,1:T(8,128)S(1)}, f32[128,16]{0,1:T(8,128)S(1)}, u32[]{:S(2)}, u32[]{:S(2)}) collective-permute-start(f32[128,16]{0,1:T(8,128)S(1)} %get-tuple-element.11), channel_id=1, source_target_pairs={{0,3},{1,0},{2,1},{3,2},{4,7},{5,4},{6,5},{7,6},{8,11},{9,8},{10,9... | collective-permute-start | bytes 24584 | tf_op jit(solution)/shard_map/ppermute | solution.py:11
  136.2 4.0 %collective-permute-start.19 = (f32[128,16]{0,1:T(8,128)S(1)}, f32[128,16]{0,1:T(8,128)S(1)}, u32[]{:S(2)}, u32[]{:S(2)}) collective-permute-start(f32[128,16]{0,1:T(8,128)S(1)} %get-tuple-element.10), channel_id=1, source_target_pairs={{0,4},{4,8},{8,12},{12,16},{16,20},{20,24},{24,28},{28,0},{1,5},{5... | collective-permute-start | bytes 24584 | tf_op jit(solution)/shard_map/ppermute | solution.py:11
  136.2 4.0 %collective-permute-start.20 = (f32[128,16]{0,1:T(8,128)S(1)}, f32[128,16]{0,1:T(8,128)S(1)}, u32[]{:S(2)}, u32[]{:S(2)}) collective-permute-start(f32[128,16]{0,1:T(8,128)S(1)} %get-tuple-element.9), channel_id=1, source_target_pairs={{0,28},{4,0},{8,4},{12,8},{16,12},{20,16},{24,20},{28,24},{1,29},{... | collective-permute-start | bytes 24584 | tf_op jit(solution)/shard_map/ppermute | solution.py:11
  (3 other events, 3.7 us)
